TPU v7x, 32 devices: a whole 2x2x4 slice. The times are simulated.
32 devices in a mesh: wide: 8 (over z, x), narrow: 4 (over y, core).
Axes of the slice: x: 2, y: 2, z: 4, core: 2. Of those that a mesh axis runs over, the one named last changes fastest.
Arguments:
- embeddings: bfloat16 [16384, 1024], P(('wide', 'narrow')), may hold values from -32 to 32
- valid: int32 [16384], P(('wide', 'narrow')), may hold values from 0 to 1, as said below
Outputs:
- whitened: bfloat16 [16384, 1024], P(('wide', 'narrow'))
Inputs may be any that keep to these rules, and one draw needn't show every extreme that they name: The first row of every aligned block of 16 rows has valid = 1.
All inputs are finite; a program needn't handle non-finite values.
Results may differ from a plain program's by a relative error of at most 0.001.
Values sent between devices are 32-bit elements; how exact they have to be, the bound alone decides.
No kernel may reach another device: no remote copies, remote signals or barrier semaphores. Data moves between devices by JAX's collectives and lax.ppermute only.
A program may use at most 64 MiB of HBM per device.

v0:
```python
import jax
import jax.numpy as jnp
from jax import lax
from jax.sharding import PartitionSpec as P


def shifted_scatter(gram, count_local, sums_local, center):
    return (
        gram
        - sums_local[:, None] * center[None, :]
        - center[:, None] * sums_local[None, :]
        + count_local * center[:, None] * center[None, :]
    )


def narrow_rows(term):
    return lax.psum_scatter(term, "narrow", scatter_dimension=0, tiled=True)


def on_device(embeddings, valid):
    width = embeddings.shape[1]
    narrow_count = lax.axis_size("narrow")
    row_span = width // narrow_count
    offset = lax.axis_index("narrow") * row_span
    mask_half = valid.astype(jnp.bfloat16)
    count_local = jnp.sum(valid.astype(jnp.float32))
    masked = embeddings * mask_half[:, None]
    gram = lax.dot_general(
        masked, embeddings, (((0,), (0,)), ((), ())), preferred_element_type=jnp.float32
    )
    sums_local = jnp.dot(mask_half[None, :], embeddings, preferred_element_type=jnp.float32)[0]
    count, sums = lax.psum((count_local, sums_local), ("wide", "narrow"))
    term = shifted_scatter(gram, count_local, sums_local, sums / count)
    level_rows = narrow_rows(term)
    own_rows = lax.psum(level_rows, "wide")
    center = sums / count
    cov_rows = own_rows / count
    ident_rows = (
        lax.broadcasted_iota(jnp.int32, (row_span, width), 0) + offset
        == lax.broadcasted_iota(jnp.int32, (row_span, width), 1)
    ).astype(jnp.float32)
    diag_block = lax.dynamic_slice_in_dim(cov_rows, offset, row_span, 1)
    trace_part = jnp.sum(jnp.diagonal(diag_block))
    square_part = jnp.sum(cov_rows * cov_rows)
    trace_cov, square_sum = lax.psum((trace_part, square_part), "narrow")
    ridge_add = 0.05 * trace_cov / width + 1e-06
    norm_frob = jnp.sqrt(square_sum + 2.0 * ridge_add * trace_cov + width * ridge_add * ridge_add)
    base_rows = (cov_rows + ridge_add * ident_rows) / norm_frob
    root_rows = (3.0 * ident_rows - base_rows) / 2.0
    root_full = lax.all_gather(root_rows, "narrow", axis=0, tiled=True)
    first = jnp.dot(
        base_rows, root_full, precision=lax.Precision.HIGHEST, preferred_element_type=jnp.float32
    )
    second = jnp.dot(
        first, root_full, precision=lax.Precision.HIGHEST, preferred_element_type=jnp.float32
    )
    factor = (3.0 * ident_rows - second) / 2.0
    root_rows = jnp.dot(
        factor, root_full, precision=lax.Precision.HIGHEST, preferred_element_type=jnp.float32
    )
    centered_x = embeddings.astype(jnp.float32) - center
    product = jnp.dot(
        centered_x,
        lax.all_gather(root_rows, "narrow", axis=0, tiled=True),
        precision=lax.Precision.HIGHEST,
        preferred_element_type=jnp.float32,
    )
    return (product / jnp.sqrt(norm_frob)).astype(jnp.bfloat16)


def solution(mesh):
    in_specs = (P(("wide", "narrow"), None), P(("wide", "narrow")))
    out_specs = P(("wide", "narrow"), None)
    return jax.shard_map(
        on_device, mesh=mesh, in_specs=in_specs, out_specs=out_specs, check_vma=False
    )
```

profile of v0, /device:TPU:0, one launch (start us, length us, event | category | flops | bytes accessed | tf_op | source)
XLA Modules:
  0.0 300.6 jit_solution(4755402428084836865)
XLA Ops:
  6.5 0.0 reduce-scatter.2.cloned.1.call-start
  6.5 0.7 convert_element_type.14
  7.2 1.3 convert_reduce_fusion
  8.5 1.5 fusion.11
  10.0 42.1 %all-reduce = (f32[1024]{0:T(1024)S(1)}, f32[]{:T(128)}) all-reduce(f32[1024]{0:T(1024)S(1)} %bitcast.12, f32[]{:T(128)} %convert_reduce_fusion), channel_id=1, replica_groups=mesh['wide'=8,'narrow'=4] {'wide','narrow'}, use_global_device_ids=true, to_apply=%region_0.0 | all-reduce | flops 1025 | bytes 8200 | tf_op jit(solution)/shard_map/psum | solution.py:32
  52.1 1.3 broadcast_multiply_fusion
  53.4 5.3 %multiply_add_fusion = f32[1024,1024]{1,0:T(8,128)} fusion(bf16[512,1024]{1,0:T(8,128)(2,1)} %param.2, f32[1024]{0:T(1024)S(1)} %get-tuple-element.11, f32[1024]{0:T(1024)S(1)} %bitcast.13, f32[1024]{0:T(1024)S(1)} %get-tuple-element.12, bf16[512]{0:T(512)(128)(2,1)S(1)} %convert_element_type.14), kind=kOutput, calls=%fused_computation.1 | convolution fusion | flops 1080557568 | bytes 5256192 | tf_op jit(solution)/shard_map/dot_general | solution.py:28
  58.7 0.0 reduce-scatter.2.cloned.1.call-update
  58.7 0.0 all-reduce.4.cloned.1.call-start
  58.8 44.7 %reduce-scatter.2.cloned.1.call-done = f32[256,1024]{1,0:T(8,128)} async-done(((f32[1024,1024]{1,0:T(8,128)}), f32[256,1024]{1,0:T(8,128)}) %reduce-scatter.2.cloned.1.call-update) | async-done | bytes 1048592 | tf_op jit(solution)/shard_map/reduce_scatter | solution.py:17
  103.5 0.0 all-reduce.4.cloned.1.call-update
  103.5 0.0 all-gather.3.cloned.1.call-start
  103.6 81.6 %all-reduce.4.cloned.1.call-done = f32[256,1024]{1,0:T(8,128)} async-done(((f32[256,1024]{1,0:T(8,128)}), f32[256,1024]{1,0:T(8,128)}) %all-reduce.4.cloned.1.call-update) | async-done | bytes 1048592 | tf_op jit(solution)/shard_map/psum | solution.py:35
  185.2 2.7 multiply_reduce_fusion
  188.0 2.3 gather_fusion
  190.4 0.7 reduce_sum.28
  191.0 7.2 %all-reduce.1 = (f32[]{:T(128)}, f32[]{:T(128)}) all-reduce(f32[]{:T(128)} %get-tuple-element.9, f32[]{:T(128)} %reduce_sum.28), channel_id=1, replica_groups=mesh['wide'=8,'narrow'=4] {'narrow'}, use_global_device_ids=true, to_apply=%region_8.9 | all-reduce | flops 2 | bytes 16 | tf_op jit(solution)/shard_map/psum | solution.py:45
  200.3 1.3 fusion.7
  201.6 0.0 all-gather.3.cloned.1.call-update
  201.6 0.2 all-gather.5.cloned.1.call-start
  201.8 33.4 %all-gather.3.cloned.1.call-done = f32[1024,1024]{1,0:T(8,128)} async-done(((f32[256,1024]{1,0:T(8,128)}), f32[1024,1024]{1,0:T(8,128)}) %all-gather.3.cloned.1.call-update) | async-done | bytes 4194320 | tf_op jit(solution)/shard_map/all_gather | solution.py:50
  235.2 0.0 copy-start
  235.2 6.1 %fusion.10 = f32[256,1024]{1,0:T(8,128)S(1)} fusion(f32[1024,1024]{1,0:T(8,128)} %all-gather.3.cloned.1.call-done, f32[256,1024]{1,0:T(8,128)S(1)} %get-tuple-element.10, f32[]{:T(128)S(6)} %sqrt.6, f32[]{:T(128)S(6)} %add.45, s32[256]{0:T(256)S(1)} %iota_add_fusion), kind=kOutput, calls=%fused_computation.23 | convolution fusion | flops 3222274048 | bytes 6292488 | tf_op jit(solution)/shard_map/dot_general | solution.py:51
  241.4 0.0 copy-done
  241.4 3.7 %fusion.4 = f32[256,1024]{1,0:T(8,128)S(1)} fusion(f32[256,1024]{1,0:T(8,128)S(1)} %fusion.10, f32[1024,1024]{1,0:T(8,128)S(1)} %copy-done, s32[256]{0:T(256)S(1)} %iota_add_fusion), kind=kOutput, calls=%fused_computation.9 | convolution fusion | flops 3222274048 | bytes 6292480 | tf_op jit(solution)/shard_map/dot_general | solution.py:54
  245.1 0.0 copy-start.1
  245.2 4.7 %fusion.12 = f32[256,1024]{1,0:T(8,128)} fusion(f32[256,1024]{1,0:T(8,128)S(1)} %fusion.4, f32[1024,1024]{1,0:T(8,128)S(1)} %copy-done), kind=kOutput, calls=%fused_computation.25 | convolution fusion | flops 3221225472 | bytes 6291456 | tf_op jit(solution)/shard_map/dot_general | solution.py:58
  249.8 0.0 all-gather.5.cloned.1.call-update
  249.9 34.6 %all-gather.5.cloned.1.call-done = f32[1024,1024]{1,0:T(8,128)} async-done(((f32[256,1024]{1,0:T(8,128)}), f32[1024,1024]{1,0:T(8,128)}) %all-gather.5.cloned.1.call-update) | async-done | bytes 4194320 | tf_op jit(solution)/shard_map/all_gather | solution.py:64
  284.5 0.0 copy-done.1
  284.5 9.6 %divide_convert_fusion = bf16[512,1024]{1,0:T(8,128)(2,1)} fusion(f32[1024,1024]{1,0:T(8,128)} %all-gather.5.cloned.1.call-done, bf16[512,1024]{1,0:T(8,128)(2,1)S(1)} %copy-done.1, f32[]{:T(128)S(6)} %sqrt.7, f32[1024]{0:T(1024)S(1)} %get-tuple-element.12), kind=kOutput, calls=%fused_computation.2 | convolution fusion | flops 6444548096 | bytes 6295556 | tf_op jit(solution)/shard_map/dot_general | solution.py:62
  (4 shorter events, 0.0 us)
Async XLA Ops:
  6.5 97.0 %reduce-scatter.2.cloned.1.call-start = ((), (), s32[]{:S(2)}) async-start(), calls=%async_computation.1 | async-start | bytes 5242880 | tf_op jit(solution)/shard_map/reduce_scatter | solution.py:17
  58.7 126.5 %all-reduce.4.cloned.1.call-start = ((), (), s32[]{:S(2)}) async-start(), calls=%async_computation.2 | async-start | bytes 2097152 | tf_op jit(solution)/shard_map/psum | solution.py:35
  103.5 131.7 %all-gather.3.cloned.1.call-start = ((), (), s32[]{:S(2)}) async-start(), calls=%async_computation.3 | async-start | bytes 5242880 | tf_op jit(solution)/shard_map/all_gather | solution.py:50
  201.6 82.9 %all-gather.5.cloned.1.call-start = ((), (), s32[]{:S(2)}) async-start(), calls=%async_computation.4 | async-start | bytes 5242880 | tf_op jit(solution)/shard_map/all_gather | solution.py:64
  235.2 6.1 %copy-start = (f32[1024,1024]{1,0:T(8,128)S(1)}, f32[1024,1024]{1,0:T(8,128)}, u32[]{:S(2)}) copy-start(f32[1024,1024]{1,0:T(8,128)} %all-gather.3.cloned.1.call-done) | copy-start | bytes 12582916
  245.1 39.3 %copy-start.1 = (bf16[512,1024]{1,0:T(8,128)(2,1)S(1)}, bf16[512,1024]{1,0:T(8,128)(2,1)}, u32[]{:S(2)}) copy-start(bf16[512,1024]{1,0:T(8,128)(2,1)} %param.2) | copy-start | bytes 3145732
Sparse Core Ops, SparseCore 0:
  58.9 44.6 reduce-scatter.1
  107.0 78.1 all-reduce.3
  201.7 33.4 all-gather.2
  250.0 34.4 all-gather.4
where the time goes:
time: 301 us
  waiting for transfers between devices  194 us (64%)
  blocking collectives  49.3 us (16%)
  matrix products  30.9 us (10%)
  between operations  15.3 us (5%)
  other arithmetic  7.97 us (3%)
    psum x1, waiting for transfers between devices, on_device(): own_rows = lax.psum(level_rows, 'wide')  81.6 us
    reduce_scatter x1, waiting for transfers between devices, narrow_rows(): return lax.psum_scatter(term, 'narrow', scatter_dimension=0, tiled=True)  44.7 us
    psum x1, blocking collectives, on_device(): count, sums = lax.psum((count_local, sums_local), ('wide', 'narrow'))  42.1 us
    all_gather x1, waiting for transfers between devices, on_device(): lax.all_gather(root_rows, 'narrow', axis=0, tiled=True)  34.6 us
    all_gather x1, waiting for transfers between devices, on_device(): root_full = lax.all_gather(root_rows, 'narrow', axis=0, tiled=True)  33.4 us
    dot_general x1, matrix products, on_device(): jnp.dot(centered_x, lax.all_gather(root_rows, 'narrow', axis=0, tiled=Tru...  9.62 us
    psum x1, blocking collectives, on_device(): trace_cov, square_sum = lax.psum((trace_part, square_part), 'narrow')  7.19 us
    dot_general x1, matrix products, on_device(): jnp.dot(base_rows, root_full, precision=lax.Precision.HIGHEST, preferred_...  6.13 us
  transfers between devices with their start and end apart: 4, of which 4 were waited for; matrix products, arithmetic and copies ran while one was open for 0% of the time, Pallas kernels for 0%

commit v1 on v0

--- a/solution.py
+++ b/solution.py
@@ -2,6 +2,16 @@
 import jax.numpy as jnp
 from jax import lax
 from jax.sharding import PartitionSpec as P
+
+
+def turned_line(x, axis, along):
+    count = lax.axis_size(axis)
+    held, shards = (x, [x])
+    for _ in range(count - 1):
+        held = lax.ppermute(held, axis, [(i, (i + 1) % count) for i in range(count)])
+        shards.insert(0, held)
+    line = jnp.concatenate(shards, axis=along)
+    return jnp.roll(line, (lax.axis_index(axis) + 1) * x.shape[along], axis=along)
 
 
 def shifted_scatter(gram, count_local, sums_local, center):
@@ -47,7 +57,7 @@
     norm_frob = jnp.sqrt(square_sum + 2.0 * ridge_add * trace_cov + width * ridge_add * ridge_add)
     base_rows = (cov_rows + ridge_add * ident_rows) / norm_frob
     root_rows = (3.0 * ident_rows - base_rows) / 2.0
-    root_full = lax.all_gather(root_rows, "narrow", axis=0, tiled=True)
+    root_full = turned_line(root_rows, "narrow", 0)
     first = jnp.dot(
         base_rows, root_full, precision=lax.Precision.HIGHEST, preferred_element_type=jnp.float32
     )

time: 301 us -> 310 us (1.030)
  waiting for transfers between devices: 194 us -> 203 us
    ppermute x0 -> x3, waiting for transfers between devices: none -> 42.8 us  [turned_line(): lax.ppermute(held, axis, [(i, (i + 1) % count) for i in range(count)])]
    all_gather x1 -> x0, waiting for transfers between devices: 33.4 us -> none  [on_device(): root_full = lax.all_gather(root_rows, 'narrow', axis=0, tiled=True)]
  transfers between devices with their start and end apart: 4 -> 6, of which waited for: 4 -> 6; matrix products, arithmetic and copies ran while one was open for 0% -> 0% of each run, Pallas kernels for 0% -> 0%
where the time goes in v1:
time: 310 us; the launch traced here: 309 us
  waiting for transfers between devices  203 us (65%)
  blocking collectives  49.3 us (16%)
  matrix products  28.6 us (9%)
  between operations  15.4 us (5%)
  other arithmetic  7.61 us (2%)
  local copies, waits for them, and re-layouts  5.24 us (2%)
    psum x1, waiting for transfers between devices, on_device(): own_rows = lax.psum(level_rows, 'wide')  81.7 us
    reduce_scatter x1, waiting for transfers between devices, narrow_rows(): return lax.psum_scatter(term, 'narrow', scatter_dimension=0, tiled=True)  44.7 us
    ppermute x3, waiting for transfers between devices, turned_line(): lax.ppermute(held, axis, [(i, (i + 1) % count) for i in range(count)])  42.8 us
    psum x1, blocking collectives, on_device(): count, sums = lax.psum((count_local, sums_local), ('wide', 'narrow'))  42.1 us
    all_gather x1, waiting for transfers between devices, on_device(): lax.all_gather(root_rows, 'narrow', axis=0, tiled=True)  33.6 us
    dot_general x1, matrix products, on_device(): jnp.dot(centered_x, lax.all_gather(root_rows, 'narrow', axis=0, tiled=Tru...  9.61 us
    psum x1, blocking collectives, on_device(): trace_cov, square_sum = lax.psum((trace_part, square_part), 'narrow')  7.19 us
  transfers between devices with their start and end apart: 6, of which 6 were waited for; matrix products, arithmetic and copies ran while one was open for 0% of the time, Pallas kernels for 0%

profile of v1, /device:TPU:0, one launch (start us, length us, event | category | flops | bytes accessed | tf_op | source)
XLA Modules:
  0.0 309.2 jit_solution(8714916684798740813)
XLA Ops:
  6.5 0.0 reduce-scatter.2.cloned.1.call-start
  6.5 0.7 convert_element_type.14
  7.2 1.3 convert_reduce_fusion
  8.5 1.5 fusion.23
  10.0 42.1 %all-reduce = (f32[1024]{0:T(1024)S(1)}, f32[]{:T(128)}) all-reduce(f32[1024]{0:T(1024)S(1)} %bitcast.9, f32[]{:T(128)} %convert_reduce_fusion), channel_id=1, replica_groups=mesh['wide'=8,'narrow'=4] {'wide','narrow'}, use_global_device_ids=true, to_apply=%region_0.0 | all-reduce | flops 1025 | bytes 8200 | tf_op jit(solution)/shard_map/psum | solution.py:42
  52.1 1.3 broadcast_multiply_fusion
  53.4 5.3 %multiply_add_fusion = f32[1024,1024]{1,0:T(8,128)} fusion(bf16[512,1024]{1,0:T(8,128)(2,1)} %param.2, f32[1024]{0:T(1024)S(1)} %get-tuple-element.11, f32[1024]{0:T(1024)S(1)} %bitcast.10, f32[1024]{0:T(1024)S(1)} %get-tuple-element.12, bf16[512]{0:T(512)(128)(2,1)S(1)} %convert_element_type.14), kind=kOutput, calls=%fused_computation.1 | convolution fusion | flops 1080557568 | bytes 5256192 | tf_op jit(solution)/shard_map/dot_general | solution.py:38
  58.7 0.0 reduce-scatter.2.cloned.1.call-update
  58.7 0.0 all-reduce.4.cloned.1.call-start
  58.8 44.7 %reduce-scatter.2.cloned.1.call-done = f32[256,1024]{1,0:T(8,128)} async-done(((f32[1024,1024]{1,0:T(8,128)}), f32[256,1024]{1,0:T(8,128)}) %reduce-scatter.2.cloned.1.call-update) | async-done | bytes 1048592 | tf_op jit(solution)/shard_map/reduce_scatter | solution.py:27
  103.5 0.0 all-reduce.4.cloned.1.call-update
  103.5 0.0 all-gather.2.cloned.1.call-start
  103.6 81.7 %all-reduce.4.cloned.1.call-done = f32[256,1024]{1,0:T(8,128)} async-done(((f32[256,1024]{1,0:T(8,128)}), f32[256,1024]{1,0:T(8,128)}) %all-reduce.4.cloned.1.call-update) | async-done | bytes 1048592 | tf_op jit(solution)/shard_map/psum | solution.py:45
  185.3 2.7 multiply_reduce_fusion
  188.1 2.3 gather_fusion
  190.5 0.7 reduce_sum.28
  191.1 7.2 %all-reduce.1 = (f32[]{:T(128)}, f32[]{:T(128)}) all-reduce(f32[]{:T(128)} %get-tuple-element.9, f32[]{:T(128)} %reduce_sum.28), channel_id=1, replica_groups=mesh['wide'=8,'narrow'=4] {'narrow'}, use_global_device_ids=true, to_apply=%region_8.9 | all-reduce | flops 2 | bytes 16 | tf_op jit(solution)/shard_map/psum | solution.py:55
  200.4 0.3 fusion.17
  200.7 0.1 collective-permute-start
  200.8 14.2 %collective-permute-done = f32[256,1024]{1,0:T(8,128)S(1)} collective-permute-done((f32[256,1024]{1,0:T(8,128)S(1)}, f32[256,1024]{1,0:T(8,128)S(1)}, u32[]{:S(2)}, u32[]{:S(2)}) %collective-permute-start) | collective-permute-done | bytes 1048608 | tf_op jit(solution)/shard_map/ppermute | solution.py:11
  215.0 0.0 collective-permute-start.1
  215.0 14.2 %collective-permute-done.1 = f32[256,1024]{1,0:T(8,128)S(1)} collective-permute-done((f32[256,1024]{1,0:T(8,128)S(1)}, f32[256,1024]{1,0:T(8,128)S(1)}, u32[]{:S(2)}, u32[]{:S(2)}) %collective-permute-start.1) | collective-permute-done | bytes 1048608 | tf_op jit(solution)/shard_map/ppermute | solution.py:11
  229.2 0.0 collective-permute-start.2
  229.2 14.3 %collective-permute-done.2 = f32[256,1024]{1,0:T(8,128)} collective-permute-done((f32[256,1024]{1,0:T(8,128)S(1)}, f32[256,1024]{1,0:T(8,128)}, u32[]{:S(2)}, u32[]{:S(2)}) %collective-permute-start.2) | collective-permute-done | bytes 1048608 | tf_op jit(solution)/shard_map/ppermute | solution.py:11
  243.6 1.3 constant_dynamic-update-slice_fusion.7
  244.9 0.1 constant_dynamic-update-slice_fusion.6
  244.9 0.1 constant_dynamic-update-slice_fusion.5
  245.0 0.3 constant_dynamic-update-slice_fusion.4
  245.3 1.3 constant_dynamic-update-slice_fusion.3
  246.6 0.1 constant_dynamic-update-slice_fusion.2
  246.7 0.1 constant_dynamic-update-slice_fusion.1
  246.8 0.3 constant_dynamic-update-slice_fusion
  247.1 3.8 %fusion.4 = f32[256,1024]{1,0:T(8,128)S(1)} fusion(f32[2048,1024]{1,0:T(8,128)S(1)} %constant_dynamic-update-slice_fusion, s32[]{:T(128)S(6)} %select_n.22, f32[256,1024]{1,0:T(8,128)S(1)} %get-tuple-element.10, f32[]{:T(128)S(6)} %sqrt.6, f32[]{:T(128)S(6)} %add.58, s32[256]{0:T(256)S(1)} %iota_add_fusion), kind=kOutput, calls=%fused_computation.6 | convolution fusion | flops 3222274048 | bytes 6292492 | tf_op jit(solution)/shard_map/dot_general | solution.py:61
  250.9 0.0 copy-start
  250.9 3.7 %fusion.12 = f32[256,1024]{1,0:T(8,128)S(1)} fusion(f32[256,1024]{1,0:T(8,128)S(1)} %fusion.4, f32[2048,1024]{1,0:T(8,128)S(1)} %constant_dynamic-update-slice_fusion, s32[]{:T(128)S(6)} %select_n.22, s32[256]{0:T(256)S(1)} %iota_add_fusion), kind=kOutput, calls=%fused_computation.15 | convolution fusion | flops 3222274048 | bytes 6292484 | tf_op jit(solution)/shard_map/dot_general | solution.py:64
  254.7 4.7 %fusion = f32[256,1024]{1,0:T(8,128)} fusion(f32[256,1024]{1,0:T(8,128)S(1)} %fusion.12, f32[2048,1024]{1,0:T(8,128)S(1)} %constant_dynamic-update-slice_fusion, s32[]{:T(128)S(6)} %select_n.22), kind=kOutput, calls=%fused_computation.2 | convolution fusion | flops 3221225472 | bytes 6291460 | tf_op jit(solution)/shard_map/dot_general | solution.py:68
  259.4 0.0 all-gather.2.cloned.1.call-update
  259.4 33.6 %all-gather.2.cloned.1.call-done = f32[1024,1024]{1,0:T(8,128)} async-done(((f32[256,1024]{1,0:T(8,128)}), f32[1024,1024]{1,0:T(8,128)}) %all-gather.2.cloned.1.call-update) | async-done | bytes 4194320 | tf_op jit(solution)/shard_map/all_gather | solution.py:74
  293.0 0.0 copy-done
  293.0 9.6 %divide_convert_fusion = bf16[512,1024]{1,0:T(8,128)(2,1)} fusion(f32[1024,1024]{1,0:T(8,128)} %all-gather.2.cloned.1.call-done, bf16[512,1024]{1,0:T(8,128)(2,1)S(1)} %copy-done, f32[]{:T(128)S(6)} %sqrt.7, f32[1024]{0:T(1024)S(1)} %get-tuple-element.12), kind=kOutput, calls=%fused_computation.8 | convolution fusion | flops 6444548096 | bytes 6295556 | tf_op jit(solution)/shard_map/dot_general | solution.py:72
  (4 shorter events, 0.0 us)
Async XLA Ops:
  6.5 97.0 %reduce-scatter.2.cloned.1.call-start = ((), (), s32[]{:S(2)}) async-start(), calls=%async_computation.1 | async-start | bytes 5242880 | tf_op jit(solution)/shard_map/reduce_scatter | solution.py:27
  58.7 126.6 %all-reduce.4.cloned.1.call-start = ((), (), s32[]{:S(2)}) async-start(), calls=%async_computation.2 | async-start | bytes 2097152 | tf_op jit(solution)/shard_map/psum | solution.py:45
  103.5 189.5 %all-gather.2.cloned.1.call-start = ((), (), s32[]{:S(2)}) async-start(), calls=%async_computation.3 | async-start | bytes 5242880 | tf_op jit(solution)/shard_map/all_gather | solution.py:74
  200.7 14.3 %collective-permute-start = (f32[256,1024]{1,0:T(8,128)S(1)}, f32[256,1024]{1,0:T(8,128)S(1)}, u32[]{:S(2)}, u32[]{:S(2)}) collective-permute-start(f32[256,1024]{1,0:T(8,128)S(1)} %fusion.17), channel_id=1, source_target_pairs={{0,1},{1,2},{2,3},{3,0},{4,5},{5,6},{6,7},{7,4},{8,9},{9,10},{10,1... | collective-permute-start | bytes 3145736 | tf_op jit(solution)/shard_map/ppermute | solution.py:11
  215.0 14.2 %collective-permute-start.1 = (f32[256,1024]{1,0:T(8,128)S(1)}, f32[256,1024]{1,0:T(8,128)S(1)}, u32[]{:S(2)}, u32[]{:S(2)}) collective-permute-start(f32[256,1024]{1,0:T(8,128)S(1)} %collective-permute-done), channel_id=1, source_target_pairs={{0,1},{1,2},{2,3},{3,0},{4,5},{5,6},{6,7},{7,4},{8,9},{9,10},{10,1... | collective-permute-start | bytes 3145736 | tf_op jit(solution)/shard_map/ppermute | solution.py:11
  229.2 14.3 %collective-permute-start.2 = (f32[256,1024]{1,0:T(8,128)S(1)}, f32[256,1024]{1,0:T(8,128)}, u32[]{:S(2)}, u32[]{:S(2)}) collective-permute-start(f32[256,1024]{1,0:T(8,128)S(1)} %collective-permute-done.1), channel_id=1, source_target_pairs={{0,1},{1,2},{2,3},{3,0},{4,5},{5,6},{6,7},{7,4},{8,9},{9,10},{10,1... | collective-permute-start | bytes 3145736 | tf_op jit(solution)/shard_map/ppermute | solution.py:11
  250.9 42.1 %copy-start = (bf16[512,1024]{1,0:T(8,128)(2,1)S(1)}, bf16[512,1024]{1,0:T(8,128)(2,1)}, u32[]{:S(2)}) copy-start(bf16[512,1024]{1,0:T(8,128)(2,1)} %param.2) | copy-start | bytes 3145732
Sparse Core Ops, SparseCore 0:
  58.9 44.6 reduce-scatter.1
  107.0 78.2 all-reduce.3
  259.5 33.4 all-gather.1
